TPU v7x, 512 devices: a whole 4x4x16 slice. The times are simulated.
512 devices in a mesh: fsdp: 32 (over y, z_hi, x), tensor: 16 (over z_lo, core).
Axes of the slice: x: 4, y: 4, z: 16 (z_hi: 2, z_lo: 8; z = z_hi * 8 + z_lo), core: 2. Of those that a mesh axis runs over, the one named last changes fastest.
Arguments:
- tokens: bfloat16 [512, 9216], P(None, 'tensor'), may hold values from -800 to 800
- ln_gain: bfloat16 [9216], P('tensor'), may hold values from 0.099609375 to 1.8984375
- ln_bias: bfloat16 [9216], P('tensor'), may hold values from -3 to 3
- fc1_weight: bfloat16 [9216, 36864], P('tensor', 'fsdp'), may hold values from -0.0625 to 0.0625
- fc1_bias: bfloat16 [36864], P('fsdp'), may hold values from -3 to 3
- fc2_weight: bfloat16 [36864, 9216], P('fsdp', 'tensor'), may hold values from -0.03125 to 0.03125
- fc2_bias: bfloat16 [9216], P('tensor'), may hold values from -3 to 3
- update_step: float32 [1], replicated, may hold values from -0.004 to 0.004
- perturb_scale: float32 [1], replicated, may hold values from 0.002 to 0.008
- step_seeds: int32 [2], replicated, may hold values from 0 to 16777215
- hash_mults: int32 [3], replicated, may hold values from 65537 to 16777215
Outputs:
- branch_plus: bfloat16 [512, 9216], P('fsdp', 'tensor')
- branch_minus: bfloat16 [512, 9216], P('fsdp', 'tensor')
Inputs may be any that keep to these rules, and one draw needn't show every extreme that they name: `step_seeds`: the previous step's seed, then this step's. `hash_mults`: three multipliers; the lowest bit is set before use.
All inputs are finite; a program needn't handle non-finite values.
Results may differ from a plain program's by a relative error of at most 0.03.
Values may be sent and summed in bfloat16 or wider, within the bound.
No kernel may reach another device: no remote copies, remote signals or barrier semaphores. Data moves between devices by JAX's collectives and lax.ppermute only.
A program may use at most 64 MiB of HBM per device.

v0:
```python
import jax
import jax.numpy as jnp
from jax import lax
from jax.sharding import PartitionSpec as P

D = 9216
FF = 36864


def shift_xor(hashed, amount):
    return hashed ^ lax.shift_right_logical(hashed, jnp.int32(amount))


def hashed_noise(param_index, seed_value, hash_mults):
    mult_a = hash_mults[0] | 1
    mult_b = hash_mults[1] | 1
    mult_c = hash_mults[2] | 1
    hashed = param_index * mult_a + seed_value * mult_b
    hashed = shift_xor(hashed, 16)
    hashed = hashed * mult_c
    hashed = shift_xor(hashed, 13)
    hashed = hashed * mult_a
    hashed = shift_xor(hashed, 16)
    fraction = (hashed & 16777215).astype(jnp.float32) * (1.0 / 16777216.0)
    return (fraction - 0.5) * 3.4641016151377544


def new_weights(weight, param_index, update_step, perturb_scale, step_seeds, hash_mults):
    updated = (
        weight.astype(jnp.float32)
        - update_step[0] * hashed_noise(param_index, step_seeds[0], hash_mults)
    ).astype(jnp.bfloat16)
    updated = lax.optimization_barrier(updated)
    updated_f = updated.astype(jnp.float32)
    shift_term = perturb_scale[0] * hashed_noise(param_index, step_seeds[1], hash_mults)
    return (
        (updated_f + shift_term).astype(jnp.bfloat16),
        (updated_f - shift_term).astype(jnp.bfloat16),
    )


def body(
    tokens,
    ln_gain,
    ln_bias,
    fc1_weight,
    fc1_bias,
    fc2_weight,
    fc2_bias,
    update_step,
    perturb_scale,
    step_seeds,
    hash_mults,
):
    feat_local = tokens.shape[1]
    unit_local = fc1_weight.shape[1]
    values = tokens.astype(jnp.float32)
    totals = lax.psum(jnp.sum(values, axis=1), "tensor")
    row_mean = (totals / D)[:, None]
    centered = values - row_mean
    squares = lax.psum(jnp.sum(centered * centered, axis=1), "tensor")
    row_var = (squares / D)[:, None]
    normed = (
        centered * lax.rsqrt(row_var + 1e-05) * ln_gain.astype(jnp.float32)
        + ln_bias.astype(jnp.float32)
    ).astype(jnp.bfloat16)
    feat_ids = lax.axis_index("tensor") * feat_local + jnp.arange(feat_local, dtype=jnp.int32)
    unit_ids = lax.axis_index("fsdp") * unit_local + jnp.arange(unit_local, dtype=jnp.int32)
    first_index = feat_ids[:, None] * FF + unit_ids[None, :]
    plus_one, minus_one = new_weights(
        fc1_weight, first_index, update_step, perturb_scale, step_seeds, hash_mults
    )
    partial_plus = jnp.dot(normed, plus_one, preferred_element_type=jnp.float32)
    partial_minus = jnp.dot(normed, minus_one, preferred_element_type=jnp.float32)
    bias_one = fc1_bias.astype(jnp.float32)
    sum_plus, sum_minus = (
        lax.psum(partial_plus.astype(jnp.bfloat16), "tensor").astype(jnp.float32),
        lax.psum(partial_minus.astype(jnp.bfloat16), "tensor").astype(jnp.float32),
    )
    hidden_plus = jax.nn.relu(sum_plus + bias_one).astype(jnp.bfloat16)
    hidden_minus = jax.nn.relu(sum_minus + bias_one).astype(jnp.bfloat16)
    second_index = D * FF + unit_ids[:, None] * D + feat_ids[None, :]
    plus_two, minus_two = new_weights(
        fc2_weight, second_index, update_step, perturb_scale, step_seeds, hash_mults
    )
    summed = lax.psum_scatter(
        jnp.concatenate(
            [
                jnp.dot(hidden_plus, plus_two, preferred_element_type=jnp.float32),
                jnp.dot(hidden_minus, minus_two, preferred_element_type=jnp.float32),
            ],
            axis=1,
        ).astype(jnp.bfloat16),
        "fsdp",
        scatter_dimension=0,
        tiled=True,
    ).astype(jnp.float32)
    bias_two = fc2_bias.astype(jnp.float32)
    branch_plus = (summed[:, :feat_local] + bias_two).astype(jnp.bfloat16)
    branch_minus = (summed[:, feat_local:] + bias_two).astype(jnp.bfloat16)
    return (branch_plus, branch_minus)


def solution(mesh):
    in_specs = (
        P(None, "tensor"),
        P("tensor"),
        P("tensor"),
        P("tensor", "fsdp"),
        P("fsdp"),
        P("fsdp", "tensor"),
        P("tensor"),
        P(),
        P(),
        P(),
        P(),
    )
    out_specs = (P("fsdp", "tensor"), P("fsdp", "tensor"))
    return jax.shard_map(body, mesh=mesh, in_specs=in_specs, out_specs=out_specs, check_vma=False)
```

profile of v0, /device:TPU:1, one launch (start us, length us, event | category | flops | bytes accessed | tf_op | source)
XLA Modules:
  0.0 657.9 jit_solution(10783687590641612165)
XLA Ops:
  7.2 0.0 all-reduce.3.cloned.1.call-start
  7.2 1.3 fusion.107
  10.4 1.3 fusion.106
  13.1 3.2 fusion.35
  16.8 0.1 convert_reduce_fusion
  17.0 51.4 %psum.28 = f32[512]{0:T(512)S(1)} all-reduce(f32[512]{0:T(512)S(1)} %convert_reduce_fusion), channel_id=1, replica_groups=mesh['fsdp'=32,'tensor'=16] {'tensor'}, use_global_device_ids=true, to_apply=%region_1.0 | all-reduce | flops 512 | bytes 4096 | tf_op jit(solution)/shard_map/psum | solution.py:58
  68.3 0.2 fusion.72
  68.5 50.4 %psum.29 = f32[512]{0:T(512)S(1)} all-reduce(f32[512]{0:T(512)S(1)} %fusion.72), channel_id=1, replica_groups=mesh['fsdp'=32,'tensor'=16] {'tensor'}, use_global_device_ids=true, to_apply=%region_3.0 | all-reduce | flops 512 | bytes 4096 | tf_op jit(solution)/shard_map/psum | solution.py:61
  119.6 3.4 convolution_convert_fusion
  123.0 3.3 convolution_convert_fusion.1
  126.3 0.0 all-reduce.3.cloned.1.call-update
  126.4 0.2 reduce-scatter.4.cloned.1.call-start
  126.6 1.0 copy-done.1
  127.7 1.8 fusion.34
  129.5 199.1 %all-reduce.3.cloned.1.call-done = (bf16[512,1152]{1,0:T(8,128)(2,1)}, bf16[512,1152]{1,0:T(8,128)(2,1)}) async-done(((bf16[512,1152]{1,0:T(8,128)(2,1)}, bf16[512,1152]{1,0:T(8,128)(2,1)}), (bf16[512,1152]{1,0:T(8,128)(2,1)}, bf16[512,1152]{1,0:T(8,128)(2,1)})) %all-reduce.3.cloned.1.call-update) | async-done | bytes 2359312 | tf_op jit(solution)/shard_map/psum | solution.py:78
  328.6 3.6 fusion.66
  332.2 2.1 fusion.69
  334.3 0.1 pad_maximum_fusion
  334.4 1.4 copy.17
  335.9 312.6 %reduce-scatter.4.cloned.1.call-done = bf16[16,1152]{1,0:T(8,128)(2,1)} async-done(((bf16[512,1152]{1,0:T(8,128)(2,1)}), bf16[16,1152]{1,0:T(8,128)(2,1)}) %reduce-scatter.4.cloned.1.call-update) | async-done | bytes 36880
  648.5 1.0 copy.18
  649.5 0.1 fusion.80
  649.6 0.7 copy.15
  650.4 0.7 copy.16
  (25 shorter events, 0.1 us)
Async XLA Ops:
  7.2 321.4 %all-reduce.3.cloned.1.call-start = ((), (), s32[]{:S(2)}) async-start(), calls=%async_computation.2 | async-start | bytes 4718592 | tf_op jit(solution)/shard_map/psum | solution.py:78
  13.0 3.8 copy-start
  13.1 106.5 %copy-start.3 = (bf16[576]{0:T(1024)(128)(2,1)S(1)}, bf16[576]{0:T(1024)(128)(2,1)}, u32[]{:S(2)}) copy-start(bf16[576]{0:T(1024)(128)(2,1)} %param.12) | copy-start | bytes 3460
  13.1 106.6 %copy-start.4 = (bf16[576]{0:T(1024)(128)(2,1)S(1)}, bf16[576]{0:T(1024)(128)(2,1)}, u32[]{:S(2)}) copy-start(bf16[576]{0:T(1024)(128)(2,1)} %param.13) | copy-start | bytes 3460
  126.3 1.3 copy-start.1
  126.4 522.1 %reduce-scatter.4.cloned.1.call-start = ((), (), s32[]{:S(2)}) async-start(), calls=%async_computation.1 | async-start | bytes 1216512
  127.7 1.8 copy-start.2
  328.6 3.6 copy-start.6
  334.4 1.4 copy-start.5
Sparse Core Ops, SparseCore 0:
  126.5 202.0 all-reduce.2
  336.0 312.4 reduce-scatter.3
where the time goes:
time: 658 us
  waiting for transfers between devices  512 us (78%)
  blocking collectives  102 us (16%)
  between operations  18.6 us (3%)
  matrix products  12.4 us (2%)
  local copies, waits for them, and re-layouts  7.57 us (1%)
    unnamed x3, waiting for transfers between devices  313 us
    psum x1, waiting for transfers between devices, body(): lax.psum(partial_minus.astype(jnp.bfloat16), 'tensor').astype(jnp.float32)  199 us
    psum x1, blocking collectives, body(): totals = lax.psum(jnp.sum(values, axis=1), 'tensor')  51.4 us
    psum x1, blocking collectives, body(): squares = lax.psum(jnp.sum(centered * centered, axis=1), 'tensor')  50.4 us
  transfers between devices with their start and end apart: 2, of which 2 were waited for; matrix products, arithmetic and copies ran while one was open for 0% of the time, Pallas kernels for 0%

commit v1 on v0

--- a/solution.py
+++ b/solution.py
@@ -73,9 +73,13 @@
     partial_plus = jnp.dot(normed, plus_one, preferred_element_type=jnp.float32)
     partial_minus = jnp.dot(normed, minus_one, preferred_element_type=jnp.float32)
     bias_one = fc1_bias.astype(jnp.float32)
+
+    def handle_the_slot(u_in):
+        return jnp.sum(lax.all_gather(u_in, "tensor"), axis=0)
+
     sum_plus, sum_minus = (
         lax.psum(partial_plus.astype(jnp.bfloat16), "tensor").astype(jnp.float32),
-        lax.psum(partial_minus.astype(jnp.bfloat16), "tensor").astype(jnp.float32),
+        handle_the_slot(partial_minus.astype(jnp.bfloat16)).astype(jnp.float32),
     )
     hidden_plus = jax.nn.relu(sum_plus + bias_one).astype(jnp.bfloat16)
     hidden_minus = jax.nn.relu(sum_minus + bias_one).astype(jnp.bfloat16)

time: 658 us -> 871 us (1.32)
  waiting for transfers between devices: 512 us -> 712 us
  other arithmetic: 5.64 us -> 19.2 us
    all_gather x0 -> x1, waiting for transfers between devices: none -> 204 us  [handle_the_slot(): return jnp.sum(lax.all_gather(u_in, 'tensor'), axis=0)]
    reduce_sum x0 -> x1, other arithmetic: none -> 10.1 us  [handle_the_slot(): return jnp.sum(lax.all_gather(u_in, 'tensor'), axis=0)]
    unnamed x3 -> x4, waiting for transfers between devices: 313 us -> 316 us
  transfers between devices with their start and end apart: 2 -> 3, of which waited for: 2 -> 3; matrix products, arithmetic and copies ran while one was open for 0% -> 1% of each run, Pallas kernels for 0% -> 0%
where the time goes in v1:
time: 871 us; the launch traced here: 870 us
  waiting for transfers between devices  712 us (82%)
  blocking collectives  102 us (12%)
  other arithmetic  19.2 us (2%)
  between operations  18.4 us (2%)
  matrix products  12.3 us (1%)
    unnamed x4, waiting for transfers between devices  316 us
    all_gather x1, waiting for transfers between devices, handle_the_slot(): return jnp.sum(lax.all_gather(u_in, 'tensor'), axis=0)  204 us
    psum x1, waiting for transfers between devices, body(): lax.psum(partial_plus.astype(jnp.bfloat16), 'tensor').astype(jnp.float32)  192 us
    psum x1, blocking collectives, body(): totals = lax.psum(jnp.sum(values, axis=1), 'tensor')  51.4 us
    psum x1, blocking collectives, body(): squares = lax.psum(jnp.sum(centered * centered, axis=1), 'tensor')  50.4 us
  transfers between devices with their start and end apart: 3, of which 3 were waited for; matrix products, arithmetic and copies ran while one was open for 1% of the time, Pallas kernels for 0%

profile of v1, /device:TPU:1, one launch (start us, length us, event | category | flops | bytes accessed | tf_op | source)
XLA Modules:
  0.0 870.5 jit_solution(14308724795223032410)
XLA Ops:
  8.6 1.3 fusion.106
  9.9 1.4 fusion.107
  14.5 1.2 convert_reduce_fusion
  15.7 51.4 %psum.21 = f32[512]{0:T(512)S(1)} all-reduce(f32[512]{0:T(512)S(1)} %convert_reduce_fusion), channel_id=1, replica_groups=mesh['fsdp'=32,'tensor'=16] {'tensor'}, use_global_device_ids=true, to_apply=%region_1.0 | all-reduce | flops 512 | bytes 4096 | tf_op jit(solution)/shard_map/psum | solution.py:58
  67.0 1.3 fusion.72
  68.3 50.4 %psum.22 = f32[512]{0:T(512)S(1)} all-reduce(f32[512]{0:T(512)S(1)} %fusion.72), channel_id=1, replica_groups=mesh['fsdp'=32,'tensor'=16] {'tensor'}, use_global_device_ids=true, to_apply=%region_3.0 | all-reduce | flops 512 | bytes 4096 | tf_op jit(solution)/shard_map/psum | solution.py:61
  118.7 0.7 convert_element_type.91
  119.4 0.7 convert_element_type.92
  120.1 3.1 fusion.35
  123.2 3.3 convolution_convert_fusion.1
  126.7 3.4 convolution_convert_fusion
  130.0 0.2 reduce-scatter.4.cloned.1.call-start
  130.3 1.8 fusion.34
  132.2 191.8 %all-reduce.2.cloned.1.call-done = bf16[512,1152]{1,0:T(8,128)(2,1)} async-done(((bf16[512,1152]{1,0:T(8,128)(2,1)}), bf16[512,1152]{1,0:T(8,128)(2,1)}) %all-reduce.2.cloned.1.call-update) | async-done | bytes 1179664 | tf_op jit(solution)/shard_map/psum | solution.py:81
  324.0 3.5 fusion.66
  327.4 203.7 %all-gather.3.cloned.1.call-done = bf16[8192,1152]{1,0:T(8,128)(2,1)} async-done(((bf16[512,1152]{1,0:T(8,128)(2,1)}), bf16[8192,1152]{1,0:T(8,128)(2,1)}) %all-gather.3.cloned.1.call-update) | async-done | bytes 18874384 | tf_op jit(solution)/shard_map/all_gather | solution.py:78
  531.1 10.1 %reduce_sum.32 = bf16[512,1152]{1,0:T(8,128)(2,1)S(1)} reduce(bf16[16,512,1152]{2,1,0:T(8,128)(2,1)} %bitcast.8, bf16[]{:T(256)} %constant.60.clone.1), dimensions={0}, to_apply=%region_5.0 | reduce | flops 8847360 | bytes 20054018 | tf_op jit(solution)/shard_map/reduce_sum | solution.py:78
  541.2 2.1 fusion.69
  543.5 1.4 copy.17
  544.9 316.4 %reduce-scatter.4.cloned.1.call-done = bf16[16,1152]{1,0:T(8,128)(2,1)} async-done(((bf16[512,1152]{1,0:T(8,128)(2,1)}), bf16[16,1152]{1,0:T(8,128)(2,1)}) %reduce-scatter.4.cloned.1.call-update) | async-done | bytes 36880
  861.3 1.0 copy.18
  862.3 0.1 fusion.80
  862.5 0.7 copy.16
  863.2 0.7 copy.15
  (23 shorter events, 0.3 us)
Async XLA Ops:
  7.2 116.0 %copy-start = (bf16[512,576]{0,1:T(8,128)(2,1)S(1)}, bf16[512,576]{0,1:T(8,128)(2,1)}, u32[]{:S(2)}) copy-start(bf16[512,576]{0,1:T(8,128)(2,1)} %param.11) | copy-start | bytes 1769476
  7.2 316.8 %all-reduce.2.cloned.1.call-start = ((), (), s32[]{:S(2)}) async-start(), calls=%async_computation.1 | async-start | bytes 2359296 | tf_op jit(solution)/shard_map/psum | solution.py:81
  126.6 3.7 copy-start.2
  126.6 3.7 copy-start.1
  126.6 404.5 %all-gather.3.cloned.1.call-start = ((), (), s32[]{:S(2)}) async-start(), calls=%async_computation.2 | async-start | bytes 20054016 | tf_op jit(solution)/shard_map/all_gather | solution.py:78
  130.0 731.3 %reduce-scatter.4.cloned.1.call-start = ((), (), s32[]{:S(2)}) async-start(), calls=%async_computation.3 | async-start | bytes 1216512
  543.4 1.5 copy-start.3
Sparse Core Ops, SparseCore 0:
  126.7 197.2 all-reduce.1
  326.0 205.0 all-gather.2
  545.0 316.2 reduce-scatter.3
